TPU v7x, 32 devices: a whole 2x2x4 slice. The times are simulated.
32 devices in a mesh: row: 8 (over y, x, core), blk: 4 (over z).
Axes of the slice: x: 2, y: 2, z: 4, core: 2. Of those that a mesh axis runs over, the one named last changes fastest.
Arguments:
- values: bfloat16 [512, 16, 256, 256], P('row', 'blk'), may hold values from -6 to 6
- scales: bfloat16 [512, 16], P('row', 'blk'), may hold values from 0.0049743652 to 0.049804688
- pattern: int32 [512, 16], P('row', 'blk'), may hold values from 0 to 2047, as said below
- omega: bfloat16 [2048, 256, 128], P(('row', 'blk')), may hold values from -6 to 6
Outputs:
- basis: float32 [2048, 256, 128], P(('row', 'blk'))
- upper: float32 [128, 128], replicated
Inputs may be any that keep to these rules, and one draw needn't show every extreme that they name: `pattern`: A block-row of group g = r // 64 has all its column blocks in g * 256 to (g + 1) * 256 - 1. Among the 256 blocks of one device (its block-rows and its positions), at most 64 lie in one aligned run of 64 column blocks, and some run holds exactly 64.
All inputs are finite; a program needn't handle non-finite values.
Results may differ from a plain program's by a relative error of at most 0.0003.
Values may be sent and summed in bfloat16 or wider, within the bound.
A program may use at most 192 MiB of HBM per device.

v0:
```python
import jax
import jax.numpy as jnp
from jax import lax
from jax.sharding import PartitionSpec as P

BS = 256
NCB = 2048


def local(values, scales, pattern, omega):
    rows_dev, per_dev = pattern.shape
    col_dev, block_side, basis_width = omega.shape
    cycle_size = lax.axis_size("blk")
    group_cols = col_dev * cycle_size
    group_base = lax.axis_index("row") * group_cols
    block_count = rows_dev * per_dev
    flat_cols = pattern.reshape(-1) - group_base
    weights = scales.astype(jnp.float32).reshape(rows_dev, per_dev, 1, 1)
    omega_slab = lax.all_gather(omega, "blk", axis=0, tiled=True)
    picked = jnp.take(omega_slab, flat_cols, axis=0)
    picked = picked.reshape(rows_dev, per_dev, block_side, basis_width)
    products = (
        jnp.einsum("rkij,rkjc->rkic", values, picked, preferred_element_type=jnp.float32) * weights
    )
    partial_value = jnp.sum(products, axis=1)
    row_total = lax.psum(partial_value, "blk")
    row_high = lax.optimization_barrier(row_total.astype(jnp.bfloat16))
    row_low = (row_total - row_high.astype(jnp.float32)).astype(jnp.bfloat16)
    high_part = jnp.einsum("rkji,rjc->rkic", values, row_high, preferred_element_type=jnp.float32)
    low_part = jnp.einsum("rkji,rjc->rkic", values, row_low, preferred_element_type=jnp.float32)
    contrib = (high_part + low_part) * weights
    contrib = contrib.reshape(block_count, block_side, basis_width)
    select_map = (flat_cols[None, :] == jnp.arange(col_dev * lax.axis_size("blk"))[:, None]).astype(
        jnp.float32
    )
    column_total = lax.psum_scatter(
        jnp.einsum("cs,sij->cij", select_map, contrib, precision=lax.Precision.HIGHEST),
        "blk",
        scatter_dimension=0,
        tiled=True,
    )
    flat_sum = column_total.reshape(col_dev * block_side, basis_width)
    gram_local = jnp.dot(flat_sum.T, flat_sum, precision=lax.Precision.HIGHEST)
    gram = lax.psum(gram_local, ("row", "blk")) / (NCB * BS)
    lower_factor = jnp.linalg.cholesky(gram)
    solved = jax.scipy.linalg.solve_triangular(lower_factor, flat_sum.T, lower=True)
    return (solved.T.reshape(col_dev, block_side, basis_width), lower_factor.T)


def solution(mesh):
    return jax.shard_map(
        local,
        mesh=mesh,
        in_specs=(
            P("row", "blk", None, None),
            P("row", "blk"),
            P("row", "blk"),
            P(("row", "blk"), None, None),
        ),
        out_specs=(P(("row", "blk"), None, None), P()),
        check_vma=False,
    )
```

profile of v0, /device:TPU:1, one launch (start us, length us, event | category | flops | bytes accessed | tf_op | source)
XLA Modules:
  0.0 1515.9 jit_solution(17570746148987104881)
XLA Ops:
  7.2 0.0 all-gather.2.cloned.1.call-start
  7.2 0.7 all-gather.2.cloned.1.call-update
  7.9 0.0 all-reduce.3.cloned.1.call-start
  7.9 0.7 compare_and_fusion
  8.6 0.1 copy.33
  8.8 0.1 copy.32
  8.9 0.1 sub.32
  9.0 0.8 copy.36
  9.8 288.8 %all-gather.2.cloned.1.call-done = bf16[256,256,128]{2,1,0:T(8,128)(2,1)} async-done(((bf16[64,256,128]{2,1,0:T(8,128)(2,1)}), bf16[256,256,128]{2,1,0:T(8,128)(2,1)}) %all-gather.2.cloned.1.call-update) | async-done | bytes 16777232 | tf_op jit(solution)/shard_map/all_gather | solution.py:19
  298.6 15.5 %gather_fusion = bf16[256,256,128]{2,1,0:T(8,128)(2,1)} fusion(bf16[256,256,128]{2,1,0:T(8,128)(2,1)} %all-gather.2.cloned.1.call-done, s32[1024]{0:T(1024)S(1)} %pad_clamp_fusion), kind=kCustom, calls=%fused_computation | custom fusion | bytes 33555456 | tf_op jit(solution)/shard_map/jit(_take)/gather | solution.py:20
  314.1 22.4 %copy.35 = bf16[64,4,256,128]{2,3,1,0:T(8,128)(2,1)} copy(bf16[64,4,256,128]{3,2,1,0:T(8,128)(2,1)} %bitcast.41) | data formatting | bytes 33554432 | tf_op jit(solution)/shard_map/jit(_take)/gather | solution.py:20
  336.5 22.9 %multiply_reduce_fusion = f32[64,128,256]{2,1,0:T(8,128)} fusion(f32[64,4]{1,0:T(8,128)S(1)} %copy.36, bf16[64,4,256,256]{3,2,1,0:T(8,128)(2,1)} %param.4, bf16[64,4,256,128]{2,3,1,0:T(8,128)(2,1)} %copy.35, pred[64,4]{1,0:T(8,128)(4,1)S(1)} %copy.33), kind=kOutput, calls=%fused_computation.2 | convolution fusion | flops 4318035968 | bytes 58721536 | tf_op jit(solution)/shard_map/rkij,rkjc->rkic/dot_general | solution.py:23
  359.4 0.0 all-reduce.3.cloned.1.call-update
  359.5 0.2 reduce-scatter.2.cloned.1.call-start
  359.7 0.1 sub.31
  359.8 288.5 %all-reduce.3.cloned.1.call-done = f32[64,256,128]{1,2,0:T(8,128)} async-done(((f32[64,256,128]{1,2,0:T(8,128)}), f32[64,256,128]{1,2,0:T(8,128)}) %all-reduce.3.cloned.1.call-update) | async-done | bytes 8388624 | tf_op jit(solution)/shard_map/psum | solution.py:26
  648.3 4.0 convert_element_type.14
  652.3 0.0 copy-start
  652.3 2.0 copy-done
  654.3 24.7 %fusion.10 = f32[64,128,4,256]{3,1,2,0:T(8,128)} fusion(bf16[64,4,256,256]{3,2,1,0:T(8,128)(2,1)} %param.4, bf16[64,256,128]{1,2,0:T(8,128)(2,1)S(1)} %convert_element_type.14), kind=kOutput, calls=%fused_computation.11 | convolution fusion | flops 4294967296 | bytes 71303168 | tf_op jit(solution)/shard_map/rkji,rjc->rkic/dot_general | solution.py:29
  679.0 38.1 %add_multiply_fusion = f32[64,128,4,256]{3,1,2,0:T(8,128)} fusion(f32[64,128,4,256]{3,1,2,0:T(8,128)} %fusion.10, f32[64,4]{1,0:T(8,128)S(1)} %copy.36, bf16[64,4,256,256]{3,2,1,0:T(8,128)(2,1)} %param.4, f32[64,256,128]{1,2,0:T(8,128)} %all-reduce.3.cloned.1.call-done, bf16[64,256,128]{1,2,0:T(8,128)(2,1)} %copy-done), kind=kOutput, calls=%fused_computation.1 | convolution fusion | flops 4318035968 | bytes 113247232 | tf_op jit(solution)/shard_map/rkji,rjc->rkic/dot_general | solution.py:30
  717.1 31.1 %copy.38 = f32[256,256,128]{2,0,1:T(8,128)} copy(f32[256,256,128]{1,2,0:T(8,128)} %bitcast.40) | data formatting | bytes 67108864 | tf_op jit(solution)/shard_map/reshape | solution.py:32
  748.2 28.9 %fusion.13 = f32[256,256,128]{2,0,1:T(8,128)} fusion(f32[256,256,128]{2,0,1:T(8,128)} %copy.38, s32[256]{0:T(256)S(1)} %sub.31), kind=kOutput, calls=%fused_computation.16 | convolution fusion | flops 25769869312 | bytes 67109888 | tf_op jit(solution)/shard_map/cs,sij->cij/dot_general | solution.py:37
  777.1 0.0 reduce-scatter.2.cloned.1.call-update
  777.1 0.3 all-reduce.5.cloned.1.call-start
  777.3 550.8 %reduce-scatter.2.cloned.1.call-done = f32[64,256,128]{2,0,1:T(8,128)} async-done(((f32[256,256,128]{2,0,1:T(8,128)}), f32[64,256,128]{2,0,1:T(8,128)}) %reduce-scatter.2.cloned.1.call-update) | async-done | bytes 8388624 | tf_op jit(solution)/shard_map/reduce_scatter | solution.py:36
  1328.2 17.6 %convolution_bitcast_fusion = f32[128,128]{0,1:T(8,128)} fusion(f32[64,256,128]{2,0,1:T(8,128)} %reduce-scatter.2.cloned.1.call-done), kind=kOutput, calls=%fused_computation.13 | convolution fusion | flops 3221225472 | bytes 8454144 | tf_op jit(solution)/shard_map/dot_general | solution.py:43
  1345.8 0.0 all-reduce.5.cloned.1.call-update
  1345.8 122.4 %all-reduce.5.cloned.1.call-done = f32[128,128]{0,1:T(8,128)} async-done(((f32[128,128]{0,1:T(8,128)}), f32[128,128]{0,1:T(8,128)}) %all-reduce.5.cloned.1.call-update) | async-done | bytes 65552 | tf_op jit(solution)/shard_map/psum | solution.py:44
  1468.2 0.8 broadcast_multiply_fusion
  1469.0 0.1 copy.40
  1469.1 0.9 fusion.17
  1470.0 11.7 cholesky.16
  1481.7 0.6 compare_reduce_fusion
  1482.4 0.7 fusion.18
  1483.0 0.7 copy.43
  1483.8 9.8 custom-call.7
  1493.6 15.7 %fusion.3 = f32[64,256,128]{2,1,0:T(8,128)} fusion(f32[64,256,128]{2,0,1:T(8,128)} %reduce-scatter.2.cloned.1.call-done, f32[1,128,128]{1,2,0:T(8,128)S(1)} %custom-call.7), kind=kOutput, calls=%fused_computation.6 | convolution fusion | flops 3221225472 | bytes 16842752 | tf_op jit(solution)/shard_map/jit(_solve_triangular)/triangular_solve | solution.py:46
  (3 shorter events, 0.0 us)
Async XLA Ops:
  7.2 291.4 %all-gather.2.cloned.1.call-start = ((), (), s32[]{:S(2)}) async-start(), calls=%async_computation.1 | async-start | bytes 20971520 | tf_op jit(solution)/shard_map/all_gather | solution.py:19
  7.9 640.4 %all-reduce.3.cloned.1.call-start = ((), (), s32[]{:S(2)}) async-start(), calls=%async_computation.2 | async-start | bytes 16777216 | tf_op jit(solution)/shard_map/psum | solution.py:26
  359.5 968.7 %reduce-scatter.2.cloned.1.call-start = ((), (), s32[]{:S(2)}) async-start(), calls=%async_computation.3 | async-start | bytes 41943040 | tf_op jit(solution)/shard_map/reduce_scatter | solution.py:36
  652.3 2.0 copy-start
  777.1 691.1 %all-reduce.5.cloned.1.call-start = ((), (), s32[]{:S(2)}) async-start(), calls=%async_computation.4 | async-start | bytes 131072 | tf_op jit(solution)/shard_map/psum | solution.py:44
Sparse Core Ops, SparseCore 0:
  9.5 288.9 all-gather.1
  359.6 288.6 all-reduce.2
  777.2 550.9 reduce-scatter.1
  1345.9 122.2 all-reduce.4
where the time goes:
time: 1520 us
  waiting for transfers between devices  1250 us (82%)
  matrix products  148 us (10%)
  local copies, waits for them, and re-layouts  73.1 us (5%)
  other arithmetic  29.2 us (2%)
    reduce_scatter x1, waiting for transfers between devices, local(): lax.psum_scatter(jnp.einsum('cs,sij->cij', select_map, contrib, precision...  551 us
    all_gather x1, waiting for transfers between devices, local(): omega_slab = lax.all_gather(omega, 'blk', axis=0, tiled=True)  289 us
    psum x1, waiting for transfers between devices, local(): row_total = lax.psum(partial_value, 'blk')  289 us
    psum x1, waiting for transfers between devices, local(): gram = lax.psum(gram_local, ('row', 'blk')) / (NCB * BS)  122 us
    dot_general x1, matrix products, local(): jnp.einsum('rkji,rjc->rkic', values, row_low, preferred_element_type=jnp....  38.1 us
    gather x2, local copies, waits for them, and re-layouts, local(): picked = jnp.take(omega_slab, flat_cols, axis=0)  37.9 us
    reshape x1, local copies, waits for them, and re-layouts, local(): contrib = contrib.reshape(block_count, block_side, basis_width)  31.1 us
  transfers between devices with their start and end apart: 4, of which 4 were waited for; matrix products, arithmetic and copies ran while one was open for 0% of the time, Pallas kernels for 0%

commit v1 on v0

--- a/solution.py
+++ b/solution.py
@@ -23,7 +23,7 @@
         jnp.einsum("rkij,rkjc->rkic", values, picked, preferred_element_type=jnp.float32) * weights
     )
     partial_value = jnp.sum(products, axis=1)
-    row_total = lax.psum(partial_value, "blk")
+    row_total = jnp.sum(lax.all_gather(partial_value, "blk"), axis=0)
     row_high = lax.optimization_barrier(row_total.astype(jnp.bfloat16))
     row_low = (row_total - row_high.astype(jnp.float32)).astype(jnp.bfloat16)
     high_part = jnp.einsum("rkji,rjc->rkic", values, row_high, preferred_element_type=jnp.float32)

time: 1520 us -> 1810 us (1.19)
  waiting for transfers between devices: 1250 us -> 1520 us
    all_gather x0 -> x1, waiting for transfers between devices: none -> 559 us  [local(): row_total = jnp.sum(lax.all_gather(partial_value, 'blk'), axis=0)]
    psum x1 -> x0, waiting for transfers between devices: 289 us -> none  [local(): row_total = lax.psum(partial_value, 'blk')]
where the time goes in v1:
time: 1810 us
  waiting for transfers between devices  1520 us (84%)
  matrix products  146 us (8%)
  local copies, waits for them, and re-layouts  80 us (4%)
  other arithmetic  47.2 us (3%)
    all_gather x1, waiting for transfers between devices, local(): row_total = jnp.sum(lax.all_gather(partial_value, 'blk'), axis=0)  559 us
    reduce_scatter x1, waiting for transfers between devices, local(): lax.psum_scatter(jnp.einsum('cs,sij->cij', select_map, contrib, precision...  550 us
    all_gather x1, waiting for transfers between devices, local(): omega_slab = lax.all_gather(omega, 'blk', axis=0, tiled=True)  289 us
    psum x1, waiting for transfers between devices, local(): gram = lax.psum(gram_local, ('row', 'blk')) / (NCB * BS)  122 us
    dot_general x1, matrix products, local(): jnp.einsum('rkji,rjc->rkic', values, row_low, preferred_element_type=jnp....  38.2 us
    gather x2, local copies, waits for them, and re-layouts, local(): picked = jnp.take(omega_slab, flat_cols, axis=0)  37.9 us
  transfers between devices with their start and end apart: 4, of which 4 were waited for; matrix products, arithmetic and copies ran while one was open for 0% of the time, Pallas kernels for 0%

profile of v1, /device:TPU:1, one launch (start us, length us, event | category | flops | bytes accessed | tf_op | source)
XLA Modules:
  0.0 1808.9 jit_solution(18278649318235528508)
XLA Ops:
  7.2 0.0 all-gather.4.cloned.1.call-start
  7.2 0.7 all-gather.4.cloned.1.call-update
  7.9 0.0 all-gather.6.cloned.1.call-start
  7.9 0.7 compare_and_fusion
  8.6 0.1 copy.45
  8.8 0.1 copy.44
  8.9 0.1 sub.32
  9.0 0.8 copy.48
  9.8 288.8 %all-gather.4.cloned.1.call-done = bf16[256,256,128]{2,1,0:T(8,128)(2,1)} async-done(((bf16[64,256,128]{2,1,0:T(8,128)(2,1)}), bf16[256,256,128]{2,1,0:T(8,128)(2,1)}) %all-gather.4.cloned.1.call-update) | async-done | bytes 16777232 | tf_op jit(solution)/shard_map/all_gather | solution.py:19
  298.6 15.5 gather_fusion
  314.1 22.4 %copy.47 = bf16[64,4,256,128]{2,3,1,0:T(8,128)(2,1)} copy(bf16[64,4,256,128]{3,2,1,0:T(8,128)(2,1)} %bitcast.42) | data formatting | bytes 33554432 | tf_op jit(solution)/shard_map/jit(_take)/gather | solution.py:20
  336.5 22.9 %multiply_reduce_fusion = f32[64,128,256]{2,1,0:T(8,128)} fusion(f32[64,4]{1,0:T(8,128)S(1)} %copy.48, bf16[64,4,256,256]{3,2,1,0:T(8,128)(2,1)} %param.4, bf16[64,4,256,128]{2,3,1,0:T(8,128)(2,1)} %copy.47, pred[64,4]{1,0:T(8,128)(4,1)S(1)} %copy.45), kind=kOutput, calls=%fused_computation.2 | convolution fusion | flops 4318035968 | bytes 58721536 | tf_op jit(solution)/shard_map/rkij,rkjc->rkic/dot_general | solution.py:23
  359.4 9.0 copy.49
  368.4 0.0 all-gather.6.cloned.1.call-update
  368.4 0.2 reduce-scatter.2.cloned.1.call-start
  368.7 0.1 sub.31
  368.8 559.4 %all-gather.6.cloned.1.call-done = f32[256,256,128]{2,1,0:T(8,128)} async-done(((f32[64,256,128]{2,1,0:T(8,128)}), f32[256,256,128]{2,1,0:T(8,128)}) %all-gather.6.cloned.1.call-update) | async-done | bytes 33554448 | tf_op jit(solution)/shard_map/all_gather | solution.py:26
  928.2 15.9 reduce_sum.22
  944.0 6.0 convert_element_type.14
  950.1 22.9 %fusion.10 = f32[64,128,4,256]{3,1,2,0:T(8,128)} fusion(bf16[64,4,256,256]{3,2,1,0:T(8,128)(2,1)} %param.4, bf16[64,256,128]{2,1,0:T(8,128)(2,1)} %convert_element_type.14), kind=kOutput, calls=%fused_computation.11 | convolution fusion | flops 4294967296 | bytes 71303168 | tf_op jit(solution)/shard_map/rkji,rjc->rkic/dot_general | solution.py:29
  973.0 38.2 %add_multiply_fusion = f32[64,128,4,256]{3,1,2,0:T(8,128)} fusion(f32[64,128,4,256]{3,1,2,0:T(8,128)} %fusion.10, f32[64,4]{1,0:T(8,128)S(1)} %copy.48, bf16[64,4,256,256]{3,2,1,0:T(8,128)(2,1)} %param.4, f32[64,256,128]{2,1,0:T(8,128)} %reduce_sum.22, bf16[64,256,128]{2,1,0:T(8,128)(2,1)} %convert_element_type.14), kind=kOutput, calls=%fused_computation.1 | convolution fusion | flops 4318035968 | bytes 113247232 | tf_op jit(solution)/shard_map/rkji,rjc->rkic/dot_general | solution.py:30
  1011.2 31.1 %copy.53 = f32[256,256,128]{2,0,1:T(8,128)} copy(f32[256,256,128]{1,2,0:T(8,128)} %bitcast.41) | data formatting | bytes 67108864 | tf_op jit(solution)/shard_map/reshape | solution.py:32
  1042.3 28.9 %fusion.13 = f32[256,256,128]{2,0,1:T(8,128)} fusion(f32[256,256,128]{2,0,1:T(8,128)} %copy.53, s32[256]{0:T(256)S(1)} %sub.31), kind=kOutput, calls=%fused_computation.16 | convolution fusion | flops 25769869312 | bytes 67109888 | tf_op jit(solution)/shard_map/cs,sij->cij/dot_general | solution.py:37
  1071.2 0.0 reduce-scatter.2.cloned.1.call-update
  1071.2 0.3 all-reduce.2.cloned.1.call-start
  1071.4 549.7 %reduce-scatter.2.cloned.1.call-done = f32[64,256,128]{2,0,1:T(8,128)} async-done(((f32[256,256,128]{2,0,1:T(8,128)}), f32[64,256,128]{2,0,1:T(8,128)}) %reduce-scatter.2.cloned.1.call-update) | async-done | bytes 8388624 | tf_op jit(solution)/shard_map/reduce_scatter | solution.py:36
  1621.2 17.6 convolution_bitcast_fusion
  1638.8 0.0 all-reduce.2.cloned.1.call-update
  1638.8 122.4 %all-reduce.2.cloned.1.call-done = f32[128,128]{0,1:T(8,128)} async-done(((f32[128,128]{0,1:T(8,128)}), f32[128,128]{0,1:T(8,128)}) %all-reduce.2.cloned.1.call-update) | async-done | bytes 65552 | tf_op jit(solution)/shard_map/psum | solution.py:44
  1761.2 0.8 broadcast_multiply_fusion
  1762.1 0.1 copy.55
  1762.2 0.9 fusion.17
  1763.0 11.7 cholesky.16
  1774.8 0.6 compare_reduce_fusion
  1775.4 0.7 fusion.18
  1776.1 0.7 copy.58
  1776.8 9.8 custom-call.7
  1786.6 15.7 fusion.3
  (3 shorter events, 0.0 us)
Async XLA Ops:
  7.2 291.4 %all-gather.4.cloned.1.call-start = ((), (), s32[]{:S(2)}) async-start(), calls=%async_computation.1 | async-start | bytes 20971520 | tf_op jit(solution)/shard_map/all_gather | solution.py:19
  7.9 920.3 %all-gather.6.cloned.1.call-start = ((), (), s32[]{:S(2)}) async-start(), calls=%async_computation.4 | async-start | bytes 41943040 | tf_op jit(solution)/shard_map/all_gather | solution.py:26
  368.4 1252.7 %reduce-scatter.2.cloned.1.call-start = ((), (), s32[]{:S(2)}) async-start(), calls=%async_computation.2 | async-start | bytes 41943040 | tf_op jit(solution)/shard_map/reduce_scatter | solution.py:36
  1071.2 690.1 %all-reduce.2.cloned.1.call-start = ((), (), s32[]{:S(2)}) async-start(), calls=%async_computation.3 | async-start | bytes 131072 | tf_op jit(solution)/shard_map/psum | solution.py:44
Sparse Core Ops, SparseCore 0:
  9.5 288.9 all-gather.3
  368.5 559.5 all-gather.5
  1071.3 549.8 reduce-scatter.1
  1638.9 122.2 all-reduce.1
